TPU v7x, 32 devices: a whole 2x2x4 slice. The times are simulated.
32 devices in a mesh: seq: 8 (over z, y), tp: 4 (over x, core).
Axes of the slice: x: 2, y: 2, z: 4, core: 2. Of those that a mesh axis runs over, the one named last changes fastest.
Arguments:
- tokens: bfloat16 [2048, 2560], P('seq', 'tp'), may hold values from -6 to 6
- segments: int32 [8, 256], P('seq'), may hold values from 0 to 3, never falling along the last dimension, each value on 1 to 128 neighbouring positions
- routes: int32 [2048, 6], P('seq'), may hold values from 0 to 63, all different within a row; in each aligned block of 256 rows (0 to 255, 256 to 511, ...) at most 40 rows name the same one
- page_table: int32 [8, 32], P('seq'), may hold values from 0 to 31, each once within a row
- cache_pool: bfloat16 [256, 16, 1024], P('seq', None, 'tp'), may hold values from -6 to 6
- attn_gain: float32 [2560], replicated, may hold values from 0.1 to 1.9
- w_query: bfloat16 [2560, 2048], P(None, 'tp'), may hold values from -0.125 to 0.125
- w_keyval: bfloat16 [2560, 1024], P(None, 'tp'), may hold values from -0.125 to 0.125
- w_out: bfloat16 [2048, 2560], P('tp'), may hold values from -0.125 to 0.125
- ffn_gain: float32 [2560], replicated, may hold values from 0.1 to 1.9
- w_router: bfloat16 [2560, 64], replicated, may hold values from -0.125 to 0.125
- expert_gate: bfloat16 [64, 1536, 2560], P('seq', 'tp'), may hold values from -0.125 to 0.125
- expert_up: bfloat16 [64, 1536, 2560], P('seq', 'tp'), may hold values from -0.125 to 0.125
- expert_down: bfloat16 [64, 1536, 2560], P('seq', 'tp'), may hold values from -0.15625 to 0.15625
- shared_gate: bfloat16 [1536, 2560], P('tp'), may hold values from -0.125 to 0.125
- shared_up: bfloat16 [1536, 2560], P('tp'), may hold values from -0.125 to 0.125
- shared_down: bfloat16 [1536, 2560], P('tp'), may hold values from -0.15625 to 0.15625
Outputs:
- layer_out: bfloat16 [2048, 2560], P('seq', 'tp')
- cache_out: bfloat16 [256, 16, 1024], P('seq', None, 'tp')
Inputs may be any that keep to these rules, and one draw needn't show every extreme that they name: `segments`: each row is one worker's block; ids never fall along a row, every segment has 1 to 128 slots and one has exactly 128. `routes`: within the 256 tokens of one worker no expert is named more than 40 times, a bound that some block reaches. `page_table`: each row lists every page of one worker's pool once; its first 16 entries take the worker's blocks in order.
All inputs are finite; a program needn't handle non-finite values.
Results may differ from a plain program's by a relative error of at most 0.019.
Values may be sent and summed in bfloat16 or wider, within the bound.
A program may use at most 192 MiB of HBM per device.

v0:
```python
import jax
import jax.numpy as jnp
from jax import lax
from jax.sharding import PartitionSpec as P

HEAD = 128
PAGE = 16
norm_eps = 1e-05
rope_base = 500000.0


def partner(block, axis, distance):
    count = lax.axis_size(axis)
    route = []
    for low in range(count):
        high = low | 1 << distance
        if high != low and high < count:
            route += [(low, high), (high, low)]
    return lax.ppermute(block, axis, route)


def gather_all(block):
    return lax.all_gather(block, ("seq", "tp"), axis=0)


def scatter_all(whole):
    part = lax.psum_scatter(whole, "tp", scatter_dimension=2, tiled=True)
    return lax.psum_scatter(part, "seq", scatter_dimension=0, tiled=False)


def rms_scale(inputs, gain_vec):
    return (
        inputs * lax.rsqrt(jnp.mean(inputs * inputs, axis=-1, keepdims=True) + norm_eps) * gain_vec
    )


def in_segment(segment_row):
    row_order = jnp.arange(segment_row.shape[0], dtype=jnp.int32)
    before = (segment_row[:, None] == segment_row[None, :]) & (
        row_order[None, :] < row_order[:, None]
    )
    return jnp.sum(before.astype(jnp.int32), axis=1)


def rotate(inputs, position):
    half_size = inputs.shape[-1] // 2
    inv_freq = rope_base ** (-jnp.arange(half_size, dtype=jnp.float32) * 2.0 / inputs.shape[-1])
    angles = position.astype(jnp.float32)[:, None] * inv_freq[None, :]
    cosine = jnp.cos(angles)[:, None, :]
    sine_term = jnp.sin(angles)[:, None, :]
    leading = inputs[..., :half_size]
    trailing = inputs[..., half_size:]
    return jnp.concatenate(
        [leading * cosine - trailing * sine_term, trailing * cosine + leading * sine_term], axis=-1
    )


def shards(
    tokens,
    segments,
    routes,
    page_table,
    cache_pool,
    attn_gain,
    w_query,
    w_keyval,
    w_out,
    ffn_gain,
    w_router,
    expert_gate,
    expert_up,
    expert_down,
    shared_gate,
    shared_up,
    shared_down,
):
    tp_count = lax.axis_size("tp")
    seq_count = lax.axis_size("seq")
    tp_rank = lax.axis_index("tp")
    row_count = tokens.shape[0]
    col_width = tokens.shape[1]
    model_width = col_width * tp_count
    whole_rows = lax.all_gather(tokens, "tp", axis=1, tiled=True)
    residual = whole_rows.astype(jnp.float32)
    normed_in = rms_scale(residual, attn_gain).astype(jnp.bfloat16)
    segment_row = segments[0]
    position = in_segment(segment_row)
    local_heads = w_query.shape[1] // HEAD
    queries = jnp.dot(normed_in, w_query, preferred_element_type=jnp.float32).reshape(
        row_count, local_heads, HEAD
    )
    queries = rotate(queries, position).astype(jnp.bfloat16)
    keyval = jnp.dot(normed_in, w_keyval, preferred_element_type=jnp.float32)
    if w_keyval.shape[1] == HEAD:
        is_key = tp_rank % 2 == 0
        rotated = rotate(keyval.reshape(row_count, 1, HEAD), position).reshape(row_count, HEAD)
        own_half = jnp.where(is_key, rotated, keyval).astype(jnp.bfloat16)
        other_half = partner(own_half, "tp", 0)
        key_rows = jnp.where(is_key, own_half, other_half)
        values = jnp.where(is_key, other_half, own_half)
        cache_rows = own_half
    else:
        key_rows = (
            rotate(keyval[:, :HEAD].reshape(row_count, 1, HEAD), position)
            .reshape(row_count, HEAD)
            .astype(jnp.bfloat16)
        )
        values = keyval[:, HEAD:].astype(jnp.bfloat16)
        cache_rows = jnp.concatenate([key_rows, values], axis=1)
    scores = jnp.einsum(
        "qhd,kd->hqk", queries, key_rows, preferred_element_type=jnp.float32
    ) * HEAD ** (-0.5)
    row_order = jnp.arange(row_count, dtype=jnp.int32)
    allowed = (segment_row[:, None] == segment_row[None, :]) & (
        row_order[None, :] <= row_order[:, None]
    )
    weights = jnp.where(allowed[None], jnp.exp(scores), 0.0)
    attn_probs = (weights / jnp.sum(weights, axis=-1, keepdims=True)).astype(jnp.bfloat16)
    attended = jnp.einsum("hqk,kd->qhd", attn_probs, values, preferred_element_type=jnp.float32)
    attended = attended.astype(jnp.bfloat16).reshape(row_count, local_heads * HEAD)
    attn_part = jnp.dot(attended, w_out, preferred_element_type=jnp.float32)
    attn_mine = lax.psum_scatter(
        attn_part.astype(jnp.bfloat16), "tp", scatter_dimension=1, tiled=True
    )
    hidden_mine = tokens.astype(jnp.float32) + attn_mine.astype(jnp.float32)
    seq_rank = lax.axis_index("seq")
    gathered = gather_all(hidden_mine.astype(jnp.bfloat16))
    hidden_all = (
        gathered.reshape(seq_count, tp_count, row_count, col_width)
        .transpose(0, 2, 1, 3)
        .reshape(seq_count, row_count, model_width)
    )
    normed_all = rms_scale(hidden_all.astype(jnp.float32), ffn_gain).astype(jnp.bfloat16)
    top_count = routes.shape[1]
    local_experts = expert_gate.shape[0]
    expert_total = local_experts * seq_count
    capacity = (
        (row_count * top_count * 5 // (expert_total * 3) + tp_count - 1) // tp_count * tp_count
    )
    slots = local_experts * capacity
    routes_all = lax.all_gather(routes, "seq", axis=0)
    chosen = jnp.sum(
        (routes_all[:, :, :, None] == jnp.arange(expert_total, dtype=jnp.int32)).astype(
            jnp.float32
        ),
        axis=2,
    )
    logits = jnp.einsum("wtd,de->wte", normed_all, w_router, preferred_element_type=jnp.float32)
    lifted = jnp.where(chosen > 0, jnp.exp(logits), 0.0)
    route_weight = lifted / jnp.sum(lifted, axis=2, keepdims=True)
    first = seq_rank * local_experts
    named = lax.dynamic_slice_in_dim(chosen, first, local_experts, 2)
    weight_mine = lax.dynamic_slice_in_dim(route_weight, first, local_experts, 2)
    earlier = (row_order[:, None] > row_order[None, :]).astype(jnp.bfloat16)
    rank = jnp.einsum(
        "ts,wse->wte", earlier, named.astype(jnp.bfloat16), preferred_element_type=jnp.float32
    ).astype(jnp.int32)
    place = jnp.where(named > 0, rank, -1)
    hit = (
        place.transpose(0, 2, 1)[:, :, None, :]
        == jnp.arange(capacity, dtype=jnp.int32)[None, None, :, None]
    )
    select = hit.astype(jnp.bfloat16).reshape(seq_count, slots, row_count)
    slot_weight = jnp.sum(
        jnp.where(hit, weight_mine.transpose(0, 2, 1)[:, :, None, :], 0.0), axis=3
    )
    slot_rows = (
        jnp.einsum("wst,wtd->wsd", select, normed_all, preferred_element_type=jnp.float32)
        .astype(jnp.bfloat16)
        .reshape(seq_count, local_experts, capacity, model_width)
    )
    gate_out = jnp.einsum(
        "secd,efd->secf", slot_rows, expert_gate, preferred_element_type=jnp.float32
    )
    up_out = jnp.einsum("secd,efd->secf", slot_rows, expert_up, preferred_element_type=jnp.float32)
    activation = (jax.nn.silu(gate_out) * up_out * slot_weight[..., None]).astype(jnp.bfloat16)
    group_part = (
        jnp.einsum("secf,efd->secd", activation, expert_down, preferred_element_type=jnp.float32)
        .astype(jnp.bfloat16)
        .reshape(seq_count, slots, model_width)
    )
    normed_mid = lax.dynamic_index_in_dim(normed_all, seq_rank, 0, keepdims=False)
    shared_gate_out = jnp.einsum(
        "td,fd->tf", normed_mid, shared_gate, preferred_element_type=jnp.float32
    )
    shared_up_out = jnp.einsum(
        "td,fd->tf", normed_mid, shared_up, preferred_element_type=jnp.float32
    )
    shared_act = (jax.nn.silu(shared_gate_out) * shared_up_out).astype(jnp.bfloat16)
    shared_part = jnp.dot(shared_act, shared_down, preferred_element_type=jnp.float32)
    routed_part = jnp.einsum("wst,wsd->wtd", select, group_part, preferred_element_type=jnp.float32)
    is_mine = jnp.arange(seq_count, dtype=jnp.int32)[:, None, None] == seq_rank
    summand = routed_part + jnp.where(is_mine, shared_part[None], 0.0)
    output_share = scatter_all(summand.astype(jnp.bfloat16)).astype(jnp.float32)
    layer_out = (hidden_mine + output_share).astype(jnp.bfloat16)
    page_count = row_count // PAGE
    new_pages = cache_rows.reshape(page_count, PAGE, cache_rows.shape[1])
    cache_out = cache_pool.at[page_table[0, :page_count]].set(new_pages)
    return (layer_out, cache_out)


def solution(mesh):
    in_specs = (
        P("seq", "tp"),
        P("seq", None),
        P("seq", None),
        P("seq", None),
        P("seq", None, "tp"),
        P(),
        P(None, "tp"),
        P(None, "tp"),
        P("tp", None),
        P(),
        P(),
        P("seq", "tp", None),
        P("seq", "tp", None),
        P("seq", "tp", None),
        P("tp", None),
        P("tp", None),
        P("tp", None),
    )
    out_specs = (P("seq", "tp"), P("seq", None, "tp"))
    return jax.shard_map(shards, mesh=mesh, in_specs=in_specs, out_specs=out_specs, check_vma=False)
```

profile of v0, /device:TPU:0, one launch (start us, length us, event | category | flops | bytes accessed | tf_op | source)
XLA Modules:
  0.0 479.4 jit_solution(7024119431726332237)
XLA Ops:
  10.3 20.2 %all-gather.5.cloned.1.call-done = bf16[256,2560]{1,0:T(8,128)(2,1)} async-done(((bf16[256,640]{1,0:T(8,128)(2,1)}), bf16[256,2560]{1,0:T(8,128)(2,1)}) %all-gather.5.cloned.1.call-update) | async-done | bytes 1310736 | tf_op jit(solution)/shard_map/all_gather | solution.py:83
  30.5 1.7 fusion.15
  32.2 3.9 fusion.56
  36.0 1.2 reshape.242
  37.2 2.5 fusion.58
  40.7 1.4 fusion.24
  42.1 1.9 convolution_convert_fusion.2
  44.1 2.0 convolution_convert_fusion.1
  46.0 2.4 copy.76
  48.5 26.6 %reduce-scatter.10.cloned.1.call-done = bf16[640,256]{1,0:T(8,128)(2,1)} async-done(((bf16[2560,256]{1,0:T(8,128)(2,1)}), bf16[640,256]{1,0:T(8,128)(2,1)}) %reduce-scatter.10.cloned.1.call-update) | async-done | bytes 327696
  77.3 30.6 %all-gather = s32[2048,6]{0,1:T(8,128)S(1)} all-gather(s32[256,6]{0,1:T(8,128)S(1)} %copy-done.13), channel_id=2, replica_groups=mesh['seq'=8,'tp'=4] {'seq'}, dimensions={0}, use_global_device_ids=true | all-gather | bytes 55296 | tf_op jit(solution)/shard_map/all_gather | solution.py:141
  109.1 56.6 %all-gather.7.cloned.1.call-done = bf16[8192,640]{1,0:T(8,128)(2,1)} async-done(((bf16[256,640]{1,0:T(8,128)(2,1)}), bf16[8192,640]{1,0:T(8,128)(2,1)}) %all-gather.7.cloned.1.call-update) | async-done | bytes 10485776 | tf_op jit(solution)/shard_map/all_gather | solution.py:23
  165.7 6.1 %multiply_reduce_fusion = f32[8192]{0:T(1024)S(1)} fusion(bf16[8192,640]{1,0:T(8,128)(2,1)} %all-gather.7.cloned.1.call-done), kind=kLoop, calls=%fused_computation.1 | loop fusion | flops 15720448 | bytes 10518528 | tf_op jit(solution)/shard_map/reduce_sum | solution.py:33
  171.9 13.8 %copy.83 = f32[8,4,32,8,640]{4,3,1,2,0:T(8,128)} copy(bf16[8,4,32,8,640]{4,3,2,1,0:T(8,128)(2,1)} %bitcast.139) | data formatting | bytes 31457280 | tf_op jit(solution)/shard_map/convert_element_type | solution.py:133
  185.7 8.4 %multiply_convert_fusion = bf16[8,256,2560]{2,1,0:T(8,128)(2,1)S(1)} fusion(f32[8,256,2560]{2,1,0:T(8,128)} %bitcast.136, f32[2560]{0:T(1024)S(1)} %copy-done.12, f32[8,256]{1,0:T(8,128)S(1)} %add_rsqrt_fusion), kind=kLoop, calls=%fused_computation.3 | loop fusion | flops 15728640 | bytes 31475712 | tf_op jit(solution)/shard_map/convert_element_type | solution.py:133
  194.1 3.3 fusion.89
  198.5 10.5 %convolution_convert_fusion = bf16[8,320,2560]{2,1,0:T(8,128)(2,1)} fusion(pred[8,320,256]{2,1,0:T(32,128)(4,1)S(1)} %bitcast_compare_fusion, bf16[8,256,2560]{2,1,0:T(8,128)(2,1)} %copy-done.2), kind=kOutput, calls=%fused_computation.13 | convolution fusion | flops 3361996800 | bytes 24248320 | tf_op jit(solution)/shard_map/wst,wtd->wsd/dot_general | solution.py:168
  209.1 14.1 %fusion.2 = f32[8,8,40,384]{3,2,1,0:T(8,128)} fusion(bf16[8,384,2560]{2,1,0:T(8,128)(2,1)} %param.29, bf16[8,8,40,2560]{3,2,1,0:T(8,128)(2,1)} %bitcast.140), kind=kOutput, calls=%fused_computation.6 | convolution fusion | flops 5033164800 | bytes 32768000 | tf_op jit(solution)/shard_map/secd,efd->secf/dot_general | solution.py:175
  223.1 24.0 %convert_bitcast_fusion = bf16[8,8,40,2560]{3,2,0,1:T(8,128)(2,1)} fusion(bf16[8,384,2560]{2,1,0:T(8,128)(2,1)} %param.30, f32[8,8,40,384]{3,2,1,0:T(8,128)} %fusion.2, bf16[8,384,2560]{2,1,0:T(8,128)(2,1)} %param.28, bf16[8,8,40,2560]{3,2,1,0:T(8,128)(2,1)} %bitcast.141, f32[8,8,40]{2,0,1:T(8,128)S(1)} %copy.67), kind=kOutput, calls=%fused_computation.10 | convolution fusion | flops 10079764480 | bytes 61614080 | tf_op jit(solution)/shard_map/secf,efd->secd/dot_general | solution.py:178
  247.2 12.5 %copy.68 = bf16[8,8,40,2560]{3,2,1,0:T(8,128)(2,1)} copy(bf16[8,8,40,2560]{3,2,0,1:T(8,128)(2,1)} %convert_bitcast_fusion) | data formatting | bytes 26214400 | tf_op jit(solution)/shard_map/convert_element_type | solution.py:179
  259.6 2.9 fusion.31
  262.6 4.3 fusion.43
  266.9 13.5 %add_convert_fusion = bf16[8,256,2560]{2,1,0:T(8,128)(2,1)} fusion(f32[256,2560]{1,0:T(8,128)S(1)} %fusion.43, pred[8]{0:T(512)(128)(4,1)S(1)} %iota_compare_fusion.5, pred[8,320,256]{2,1,0:T(32,128)(4,1)} %copy-done.4, bf16[8,320,2560]{2,1,0:T(8,128)(2,1)} %bitcast.142), kind=kOutput, calls=%fused_computation.2 | convolution fusion | flops 3371171840 | bytes 26869768 | tf_op jit(solution)/shard_map/wst,wsd->wtd/dot_general | solution.py:191
  280.4 14.7 %copy.78 = bf16[8,256,2560]{1,0,2:T(8,128)(2,1)} copy(bf16[8,256,2560]{2,1,0:T(8,128)(2,1)} %add_convert_fusion) | data formatting | bytes 20971520
  295.0 12.4 %copy.84 = bf16[320,8,8,256]{3,1,2,0:T(8,128)(2,1)} copy(bf16[320,8,8,256]{3,2,1,0:T(8,128)(2,1)} %bitcast.138) | data formatting | bytes 20971520
  307.5 83.9 %reduce-scatter.12.cloned.1.call-done = bf16[640,2048]{1,0:T(8,128)(2,1)} async-done(((bf16[2560,2048]{1,0:T(8,128)(2,1)}), bf16[640,2048]{1,0:T(8,128)(2,1)}) %reduce-scatter.12.cloned.1.call-update) | async-done | bytes 2621456
  391.4 4.1 copy.85
  395.6 5.0 %copy.79 = bf16[8,256,640]{2,1,0:T(8,128)(2,1)} copy(bf16[8,256,640]{1,0,2:T(8,128)(2,1)} %bitcast.143) | data formatting | bytes 5242880
  403.0 1.7 copy.69
  404.6 1.7 scatter_fusion
  406.4 64.7 %reduce-scatter.8.cloned.1.call-done = bf16[1,256,640]{2,1,0:T(8,128)(2,1)} async-done(((bf16[8,256,640]{2,1,0:T(8,128)(2,1)}), bf16[1,256,640]{2,1,0:T(8,128)(2,1)}) %reduce-scatter.8.cloned.1.call-update) | async-done | bytes 327696 | tf_op jit(solution)/shard_map/reduce_scatter | solution.py:28
  471.1 1.8 fusion.48
  (70 shorter events, 10.9 us)
Async XLA Ops:
  7.2 36.9 %copy-start = (bf16[512,2560]{1,0:T(8,128)(2,1)S(1)}, bf16[512,2560]{1,0:T(8,128)(2,1)}, u32[]{:S(2)}) copy-start(bf16[512,2560]{1,0:T(8,128)(2,1)} %param.25) | copy-start | bytes 7864324
  7.2 23.3 %all-gather.5.cloned.1.call-start = ((), (), s32[]{:S(2)}) async-start(), calls=%async_computation.3 | async-start | bytes 1638400 | tf_op jit(solution)/shard_map/all_gather | solution.py:83
  7.9 67.3 %reduce-scatter.10.cloned.1.call-start = ((), (), s32[]{:S(2)}) async-start(), calls=%async_computation.6 | async-start | bytes 1638400
  10.3 27.0 %copy-start.14 = (f32[2560]{0:T(1024)S(1)}, f32[2560]{0:T(1024)}, u32[]{:S(2)}) copy-start(f32[2560]{0:T(1024)} %param.22) | copy-start | bytes 30724
  39.7 0.9 copy-start.11
  40.1 0.6 copy-start.9
  40.1 0.6 copy-start.10
  44.1 32.3 %copy-start.3 = (bf16[256,640]{1,0:T(8,128)(2,1)S(1)}, bf16[256,640]{1,0:T(8,128)(2,1)}, u32[]{:S(2)}) copy-start(bf16[256,640]{1,0:T(8,128)(2,1)} %param.17) | copy-start | bytes 983044
  46.0 31.3 %copy-start.13 = (s32[256,6]{0,1:T(8,128)S(1)}, s32[256,6]{0,1:T(8,128)}, u32[]{:S(2)}) copy-start(s32[256,6]{0,1:T(8,128)} %param.19) | copy-start | bytes 18436
  48.5 117.2 %all-gather.7.cloned.1.call-start = ((), (), s32[]{:S(2)}) async-start(), calls=%async_computation.5 | async-start | bytes 10813440 | tf_op jit(solution)/shard_map/all_gather | solution.py:23
  77.2 314.3 %reduce-scatter.12.cloned.1.call-start = ((), (), s32[]{:S(2)}) async-start(), calls=%async_computation.7 | async-start | bytes 13107200
  109.0 89.5 %copy-start.4 = (pred[8,320,256]{2,1,0:T(32,128)(4,1)}, pred[8,320,256]{2,1,0:T(32,128)(4,1)S(1)}, u32[]{:S(2)}) copy-start(pred[8,320,256]{2,1,0:T(32,128)(4,1)S(1)} %bitcast_compare_fusion) | copy-start | bytes 1966084
  171.9 13.8 %copy-start.12 = (f32[2560]{0:T(1024)S(1)}, f32[2560]{0:T(1024)}, u32[]{:S(2)}) copy-start(f32[2560]{0:T(1024)} %param.26) | copy-start | bytes 30724
  185.6 8.4 %copy-start.8 = (bf16[2560,64]{0,1:T(8,128)(2,1)S(1)}, bf16[2560,64]{0,1:T(8,128)(2,1)}, u32[]{:S(2)}) copy-start(bf16[2560,64]{0,1:T(8,128)(2,1)} %param.27) | copy-start | bytes 983044
  194.0 3.9 copy-start.2
  247.2 12.5 %copy-start.5 = (bf16[384,2560]{1,0:T(8,128)(2,1)S(1)}, bf16[384,2560]{1,0:T(8,128)(2,1)}, u32[]{:S(2)}) copy-start(bf16[384,2560]{1,0:T(8,128)(2,1)} %param.31) | copy-start | bytes 5898244
  307.5 163.6 %reduce-scatter.8.cloned.1.call-start = ((), (), s32[]{:S(2)}) async-start(), calls=%async_computation.4 | async-start | bytes 2949120 | tf_op jit(solution)/shard_map/reduce_scatter | solution.py:28
  395.6 77.3 %copy-start.1 = (bf16[512,2560]{1,0:T(8,128)(2,1)S(1)}, bf16[512,2560]{1,0:T(8,128)(2,1)}, u32[]{:S(2)}) copy-start(bf16[512,2560]{1,0:T(8,128)(2,1)} %param.25) | copy-start | bytes 7864324
  395.6 5.0 %copy-start.15 = (s32[1,32]{1,0:T(1,128)S(1)}, s32[1,32]{1,0:T(1,128)}, u32[]{:S(2)}) copy-start(s32[1,32]{1,0:T(1,128)} %param.20) | copy-start | bytes 388
  395.6 9.1 %copy-start.7 = (bf16[32,16,256]{2,1,0:T(8,128)(2,1)S(1)}, bf16[32,16,256]{2,1,0:T(8,128)(2,1)}, u32[]{:S(2)}) copy-start(bf16[32,16,256]{2,1,0:T(8,128)(2,1)} %param.21) | copy-start | bytes 786436
  406.3 66.6 %copy-start.6 = (bf16[32,16,256]{2,1,0:T(8,128)(2,1)}, bf16[32,16,256]{2,1,0:T(8,128)(2,1)S(1)}, u32[]{:S(2)}) copy-start(bf16[32,16,256]{2,1,0:T(8,128)(2,1)S(1)} %scatter_fusion) | copy-start | bytes 786436
Sparse Core Ops, SparseCore 0:
  9.6 20.8 all-gather.4
  48.6 26.5 reduce-scatter.9
  79.0 86.6 all-gather.6
  307.6 83.8 reduce-scatter.11
  400.7 70.3 reduce-scatter.7
where the time goes:
time: 481 us; the launch traced here: 479 us
  waiting for transfers between devices  253 us (53%)
  matrix products  84.5 us (18%)
  local copies, waits for them, and re-layouts  72.8 us (15%)
  blocking collectives  30.6 us (6%)
  other arithmetic  24.3 us (5%)
  between operations  14.1 us (3%)
    unnamed x7, waiting for transfers between devices  111 us
    reduce_scatter x1, waiting for transfers between devices, scatter_all(): return lax.psum_scatter(part, 'seq', scatter_dimension=0, tiled=False)  64.7 us
    all_gather x1, waiting for transfers between devices, gather_all(): return lax.all_gather(block, ('seq', 'tp'), axis=0)  56.6 us
    unnamed x38, local copies, waits for them, and re-layouts  40.6 us
    all_gather x1, blocking collectives, shards(): routes_all = lax.all_gather(routes, 'seq', axis=0)  30.6 us
    dot_general x1, matrix products, shards(): jnp.einsum('secf,efd->secd', activation, expert_down, preferred_element_t...  24 us
    all_gather x1, waiting for transfers between devices, shards(): whole_rows = lax.all_gather(tokens, 'tp', axis=1, tiled=True)  20.2 us
    dot_general x1, matrix products, shards(): jnp.einsum('secd,efd->secf', slot_rows, expert_up, preferred_element_type...  14.1 us
  transfers between devices with their start and end apart: 5, of which 5 were waited for; matrix products, arithmetic and copies ran while one was open for 2% of the time, Pallas kernels for 0%

commit v1 on v0

--- a/solution.py
+++ b/solution.py
@@ -80,7 +80,15 @@
     row_count = tokens.shape[0]
     col_width = tokens.shape[1]
     model_width = col_width * tp_count
-    whole_rows = lax.all_gather(tokens, "tp", axis=1, tiled=True)
+    peers, index, span = (lax.axis_size("tp"), lax.axis_index("tp"), tokens.shape[1])
+    right = [(i, (i + 1) % peers) for i in range(peers)]
+    whole_rows = jnp.zeros((*tokens.shape[:1], peers * span, *tokens.shape[1 + 1 :]), tokens.dtype)
+    carried = tokens
+    for step in range(peers):
+        owner = (index - step) % peers
+        whole_rows = lax.dynamic_update_slice_in_dim(whole_rows, carried, owner * span, axis=1)
+        if step < peers - 1:
+            carried = lax.ppermute(carried, "tp", right)
     residual = whole_rows.astype(jnp.float32)
     normed_in = rms_scale(residual, attn_gain).astype(jnp.bfloat16)
     segment_row = segments[0]

time: 481 us -> 477 us (level)
    all_gather x1 -> x0, waiting for transfers between devices: 20.2 us -> none  [shards(): whole_rows = lax.all_gather(tokens, 'tp', axis=1, tiled=True)]
    ppermute x0 -> x3, waiting for transfers between devices: none -> 16.3 us  [shards(): carried = lax.ppermute(carried, 'tp', right)]
    unnamed x7 -> x6, waiting for transfers between devices: 111 us -> 113 us
    unnamed x38 -> x42, local copies, waits for them, and re-layouts: 40.6 us -> 40.7 us
  transfers between devices with their start and end apart: 5 -> 7, of which waited for: 5 -> 7; matrix products, arithmetic and copies ran while one was open for 2% -> 2% of each run, Pallas kernels for 0% -> 0%
where the time goes in v1:
time: 477 us; the launch traced here: 475 us
  waiting for transfers between devices  251 us (53%)
  matrix products  81.3 us (17%)
  local copies, waits for them, and re-layouts  75 us (16%)
  blocking collectives  30.6 us (6%)
  other arithmetic  23.1 us (5%)
  between operations  14.1 us (3%)
    unnamed x6, waiting for transfers between devices  113 us
    reduce_scatter x1, waiting for transfers between devices, scatter_all(): return lax.psum_scatter(part, 'seq', scatter_dimension=0, tiled=False)  65 us
    all_gather x1, waiting for transfers between devices, gather_all(): return lax.all_gather(block, ('seq', 'tp'), axis=0)  56.6 us
    unnamed x42, local copies, waits for them, and re-layouts  40.7 us
    all_gather x1, blocking collectives, shards(): routes_all = lax.all_gather(routes, 'seq', axis=0)  30.6 us
    dot_general x1, matrix products, shards(): jnp.einsum('secf,efd->secd', activation, expert_down, preferred_element_t...  24 us
    ppermute x3, waiting for transfers between devices, shards(): carried = lax.ppermute(carried, 'tp', right)  16.3 us
    dot_general x1, matrix products, shards(): jnp.einsum('secd,efd->secf', slot_rows, expert_up, preferred_element_type...  14.1 us
  transfers between devices with their start and end apart: 7, of which 7 were waited for; matrix products, arithmetic and copies ran while one was open for 2% of the time, Pallas kernels for 0%

profile of v1, /device:TPU:0, one launch (start us, length us, event | category | flops | bytes accessed | tf_op | source)
XLA Modules:
  0.0 475.4 jit_solution(14007602383540801382)
XLA Ops:
  9.6 5.1 %collective-permute-done = bf16[256,640]{1,0:T(8,128)(2,1)S(1)} collective-permute-done((bf16[256,640]{1,0:T(8,128)(2,1)}, bf16[256,640]{1,0:T(8,128)(2,1)S(1)}, u32[]{:S(2)}, u32[]{:S(2)}) %collective-permute-start) | collective-permute-done | bytes 327712 | tf_op jit(solution)/shard_map/ppermute | solution.py:91
  15.2 5.9 %collective-permute-done.1 = bf16[256,640]{1,0:T(8,128)(2,1)S(1)} collective-permute-done((bf16[256,640]{1,0:T(8,128)(2,1)S(1)}, bf16[256,640]{1,0:T(8,128)(2,1)S(1)}, u32[]{:S(2)}, u32[]{:S(2)}) %collective-permute-start.1) | collective-permute-done | bytes 327712 | tf_op jit(solution)/shard_map/ppermute | solution.py:91
  22.4 5.3 %collective-permute-done.2 = bf16[256,640]{1,0:T(8,128)(2,1)S(1)} collective-permute-done((bf16[256,640]{1,0:T(8,128)(2,1)S(1)}, bf16[256,640]{1,0:T(8,128)(2,1)S(1)}, u32[]{:S(2)}, u32[]{:S(2)}) %collective-permute-start.2) | collective-permute-done | bytes 327712 | tf_op jit(solution)/shard_map/ppermute | solution.py:91
  28.0 1.5 fusion.58
  29.6 1.7 fusion.56
  34.3 1.4 fusion.24
  35.7 1.9 convolution_convert_fusion.2
  37.6 1.9 convolution_convert_fusion.1
  39.6 2.5 copy.76
  42.1 28.7 %reduce-scatter.10.cloned.1.call-done = bf16[640,256]{1,0:T(8,128)(2,1)} async-done(((bf16[2560,256]{1,0:T(8,128)(2,1)}), bf16[640,256]{1,0:T(8,128)(2,1)}) %reduce-scatter.10.cloned.1.call-update) | async-done | bytes 327696
  73.0 30.6 %all-gather = s32[2048,6]{0,1:T(8,128)S(1)} all-gather(s32[256,6]{0,1:T(8,128)S(1)} %copy-done.13), channel_id=2, replica_groups=mesh['seq'=8,'tp'=4] {'seq'}, dimensions={0}, use_global_device_ids=true | all-gather | bytes 55296 | tf_op jit(solution)/shard_map/all_gather | solution.py:149
  104.7 56.6 %all-gather.4.cloned.1.call-done = bf16[8192,640]{1,0:T(8,128)(2,1)} async-done(((bf16[256,640]{1,0:T(8,128)(2,1)}), bf16[8192,640]{1,0:T(8,128)(2,1)}) %all-gather.4.cloned.1.call-update) | async-done | bytes 10485776 | tf_op jit(solution)/shard_map/all_gather | solution.py:23
  161.3 6.1 %multiply_reduce_fusion = f32[8192]{0:T(1024)S(1)} fusion(bf16[8192,640]{1,0:T(8,128)(2,1)} %all-gather.4.cloned.1.call-done), kind=kLoop, calls=%fused_computation.1 | loop fusion | flops 15720448 | bytes 10518528 | tf_op jit(solution)/shard_map/reduce_sum | solution.py:33
  167.5 13.8 %copy.83 = f32[8,4,32,8,640]{4,3,1,2,0:T(8,128)} copy(bf16[8,4,32,8,640]{4,3,2,1,0:T(8,128)(2,1)} %bitcast.139) | data formatting | bytes 31457280 | tf_op jit(solution)/shard_map/convert_element_type | solution.py:141
  181.3 8.4 %multiply_convert_fusion = bf16[8,256,2560]{2,1,0:T(8,128)(2,1)S(1)} fusion(f32[8,256,2560]{2,1,0:T(8,128)} %bitcast.136, f32[2560]{0:T(1024)S(1)} %copy-done.12, f32[8,256]{1,0:T(8,128)S(1)} %add_rsqrt_fusion), kind=kLoop, calls=%fused_computation.3 | loop fusion | flops 15728640 | bytes 31475712 | tf_op jit(solution)/shard_map/convert_element_type | solution.py:141
  189.7 3.3 fusion.89
  194.1 10.5 %convolution_convert_fusion = bf16[8,320,2560]{2,1,0:T(8,128)(2,1)} fusion(pred[8,320,256]{2,1,0:T(32,128)(4,1)S(1)} %bitcast_compare_fusion, bf16[8,256,2560]{2,1,0:T(8,128)(2,1)} %copy-done.2), kind=kOutput, calls=%fused_computation.13 | convolution fusion | flops 3361996800 | bytes 24248320 | tf_op jit(solution)/shard_map/wst,wtd->wsd/dot_general | solution.py:176
  204.7 14.1 %fusion.2 = f32[8,8,40,384]{3,2,1,0:T(8,128)} fusion(bf16[8,384,2560]{2,1,0:T(8,128)(2,1)} %param.29, bf16[8,8,40,2560]{3,2,1,0:T(8,128)(2,1)} %bitcast.140), kind=kOutput, calls=%fused_computation.6 | convolution fusion | flops 5033164800 | bytes 32768000 | tf_op jit(solution)/shard_map/secd,efd->secf/dot_general | solution.py:183
  218.8 24.0 %convert_bitcast_fusion = bf16[8,8,40,2560]{3,2,0,1:T(8,128)(2,1)} fusion(bf16[8,384,2560]{2,1,0:T(8,128)(2,1)} %param.30, f32[8,8,40,384]{3,2,1,0:T(8,128)} %fusion.2, bf16[8,384,2560]{2,1,0:T(8,128)(2,1)} %param.28, bf16[8,8,40,2560]{3,2,1,0:T(8,128)(2,1)} %bitcast.141, f32[8,8,40]{2,0,1:T(8,128)S(1)} %copy.67), kind=kOutput, calls=%fused_computation.10 | convolution fusion | flops 10079764480 | bytes 61614080 | tf_op jit(solution)/shard_map/secf,efd->secd/dot_general | solution.py:186
  242.8 12.5 %copy.68 = bf16[8,8,40,2560]{3,2,1,0:T(8,128)(2,1)} copy(bf16[8,8,40,2560]{3,2,0,1:T(8,128)(2,1)} %convert_bitcast_fusion) | data formatting | bytes 26214400 | tf_op jit(solution)/shard_map/convert_element_type | solution.py:187
  255.3 2.9 fusion.31
  258.2 4.3 fusion.43
  262.5 13.5 %add_convert_fusion = bf16[8,256,2560]{2,1,0:T(8,128)(2,1)} fusion(f32[256,2560]{1,0:T(8,128)S(1)} %fusion.43, pred[8]{0:T(512)(128)(4,1)S(1)} %iota_compare_fusion.5, pred[8,320,256]{2,1,0:T(32,128)(4,1)} %copy-done.4, bf16[8,320,2560]{2,1,0:T(8,128)(2,1)} %bitcast.142), kind=kOutput, calls=%fused_computation.2 | convolution fusion | flops 3371171840 | bytes 26869768 | tf_op jit(solution)/shard_map/wst,wsd->wtd/dot_general | solution.py:199
  276.0 14.7 %copy.78 = bf16[8,256,2560]{1,0,2:T(8,128)(2,1)} copy(bf16[8,256,2560]{2,1,0:T(8,128)(2,1)} %add_convert_fusion) | data formatting | bytes 20971520
  290.7 12.4 %copy.84 = bf16[320,8,8,256]{3,1,2,0:T(8,128)(2,1)} copy(bf16[320,8,8,256]{3,2,1,0:T(8,128)(2,1)} %bitcast.138) | data formatting | bytes 20971520
  303.2 83.9 %reduce-scatter.12.cloned.1.call-done = bf16[640,2048]{1,0:T(8,128)(2,1)} async-done(((bf16[2560,2048]{1,0:T(8,128)(2,1)}), bf16[640,2048]{1,0:T(8,128)(2,1)}) %reduce-scatter.12.cloned.1.call-update) | async-done | bytes 2621456
  387.1 4.1 copy.85
  391.2 5.0 %copy.79 = bf16[8,256,640]{2,1,0:T(8,128)(2,1)} copy(bf16[8,256,640]{1,0,2:T(8,128)(2,1)} %bitcast.143) | data formatting | bytes 5242880
  398.6 1.7 copy.69
  400.3 1.7 scatter_fusion
  402.0 65.0 %reduce-scatter.8.cloned.1.call-done = bf16[1,256,640]{2,1,0:T(8,128)(2,1)} async-done(((bf16[8,256,640]{2,1,0:T(8,128)(2,1)}), bf16[1,256,640]{2,1,0:T(8,128)(2,1)}) %reduce-scatter.8.cloned.1.call-update) | async-done | bytes 327696 | tf_op jit(solution)/shard_map/reduce_scatter | solution.py:28
  467.0 1.8 fusion.48
  (82 shorter events, 14.4 us)
Async XLA Ops:
  7.2 30.5 %copy-start = (bf16[512,2560]{1,0:T(8,128)(2,1)S(1)}, bf16[512,2560]{1,0:T(8,128)(2,1)}, u32[]{:S(2)}) copy-start(bf16[512,2560]{1,0:T(8,128)(2,1)} %param.25) | copy-start | bytes 7864324
  7.2 20.9 %copy-start.16 = (f32[2560]{0:T(1024)S(1)}, f32[2560]{0:T(1024)}, u32[]{:S(2)}) copy-start(f32[2560]{0:T(1024)} %param.22) | copy-start | bytes 30724
  7.2 63.6 %reduce-scatter.10.cloned.1.call-start = ((), (), s32[]{:S(2)}) async-start(), calls=%async_computation.5 | async-start | bytes 1638400
  7.2 7.4 %collective-permute-start = (bf16[256,640]{1,0:T(8,128)(2,1)}, bf16[256,640]{1,0:T(8,128)(2,1)S(1)}, u32[]{:S(2)}, u32[]{:S(2)}) collective-permute-start(bf16[256,640]{1,0:T(8,128)(2,1)} %param.17), channel_id=1, source_target_pairs={{0,1},{1,2},{2,3},{3,0},{4,5},{5,6},{6,7},{7,4},{8,9},{9,10},{10,1... | collective-permute-start | bytes 983048 | tf_op jit(solution)/shard_map/ppermute | solution.py:91
  8.6 19.4 %copy-start.15 = (bf16[2560,256]{1,0:T(8,128)(2,1)S(1)}, bf16[2560,256]{1,0:T(8,128)(2,1)}, u32[]{:S(2)}) copy-start(bf16[2560,256]{1,0:T(8,128)(2,1)} %param.24) | copy-start | bytes 3932164
  14.6 6.5 %collective-permute-start.1 = (bf16[256,640]{1,0:T(8,128)(2,1)S(1)}, bf16[256,640]{1,0:T(8,128)(2,1)S(1)}, u32[]{:S(2)}, u32[]{:S(2)}) collective-permute-start(bf16[256,640]{1,0:T(8,128)(2,1)S(1)} %collective-permute-done), channel_id=1, source_target_pairs={{0,1},{1,2},{2,3},{3,0},{4,5},{5,6},{6,7},{7,4},{8,9},{9,10},{10,1... | collective-permute-start | bytes 983048 | tf_op jit(solution)/shard_map/ppermute | solution.py:91
  21.1 6.5 %collective-permute-start.2 = (bf16[256,640]{1,0:T(8,128)(2,1)S(1)}, bf16[256,640]{1,0:T(8,128)(2,1)S(1)}, u32[]{:S(2)}, u32[]{:S(2)}) collective-permute-start(bf16[256,640]{1,0:T(8,128)(2,1)S(1)} %collective-permute-done.1), channel_id=1, source_target_pairs={{0,1},{1,2},{2,3},{3,0},{4,5},{5,6},{6,7},{7,4},{8,9},{9,10},{10,1... | collective-permute-start | bytes 983048 | tf_op jit(solution)/shard_map/ppermute | solution.py:91
  22.3 7.2 %copy-start.14 = (bf16[2560,512]{1,0:T(8,128)(2,1)S(1)}, bf16[2560,512]{1,0:T(8,128)(2,1)}, u32[]{:S(2)}) copy-start(bf16[2560,512]{1,0:T(8,128)(2,1)} %param.23) | copy-start | bytes 7864324
  33.7 0.6 copy-start.9
  33.7 0.6 copy-start.10
  34.1 1.7 copy-start.11
  39.6 32.4 %copy-start.3 = (bf16[256,640]{1,0:T(8,128)(2,1)S(1)}, bf16[256,640]{1,0:T(8,128)(2,1)}, u32[]{:S(2)}) copy-start(bf16[256,640]{1,0:T(8,128)(2,1)} %param.17) | copy-start | bytes 983044
  39.6 33.4 %copy-start.13 = (s32[256,6]{0,1:T(8,128)S(1)}, s32[256,6]{0,1:T(8,128)}, u32[]{:S(2)}) copy-start(s32[256,6]{0,1:T(8,128)} %param.19) | copy-start | bytes 18436
  42.1 119.2 %all-gather.4.cloned.1.call-start = ((), (), s32[]{:S(2)}) async-start(), calls=%async_computation.4 | async-start | bytes 10813440 | tf_op jit(solution)/shard_map/all_gather | solution.py:23
  72.8 314.2 %reduce-scatter.12.cloned.1.call-start = ((), (), s32[]{:S(2)}) async-start(), calls=%async_computation.6 | async-start | bytes 13107200
  104.7 89.5 %copy-start.4 = (pred[8,320,256]{2,1,0:T(32,128)(4,1)}, pred[8,320,256]{2,1,0:T(32,128)(4,1)S(1)}, u32[]{:S(2)}) copy-start(pred[8,320,256]{2,1,0:T(32,128)(4,1)S(1)} %bitcast_compare_fusion) | copy-start | bytes 1966084
  167.5 13.8 %copy-start.12 = (f32[2560]{0:T(1024)S(1)}, f32[2560]{0:T(1024)}, u32[]{:S(2)}) copy-start(f32[2560]{0:T(1024)} %param.26) | copy-start | bytes 30724
  181.3 8.4 %copy-start.8 = (bf16[2560,64]{0,1:T(8,128)(2,1)S(1)}, bf16[2560,64]{0,1:T(8,128)(2,1)}, u32[]{:S(2)}) copy-start(bf16[2560,64]{0,1:T(8,128)(2,1)} %param.27) | copy-start | bytes 983044
  189.7 3.9 copy-start.2
  242.8 12.5 %copy-start.5 = (bf16[384,2560]{1,0:T(8,128)(2,1)S(1)}, bf16[384,2560]{1,0:T(8,128)(2,1)}, u32[]{:S(2)}) copy-start(bf16[384,2560]{1,0:T(8,128)(2,1)} %param.31) | copy-start | bytes 5898244
  303.1 163.9 %reduce-scatter.8.cloned.1.call-start = ((), (), s32[]{:S(2)}) async-start(), calls=%async_computation.3 | async-start | bytes 2949120 | tf_op jit(solution)/shard_map/reduce_scatter | solution.py:28
  391.2 5.0 %copy-start.17 = (s32[1,32]{1,0:T(1,128)S(1)}, s32[1,32]{1,0:T(1,128)}, u32[]{:S(2)}) copy-start(s32[1,32]{1,0:T(1,128)} %param.20) | copy-start | bytes 388
  391.2 9.1 %copy-start.7 = (bf16[32,16,256]{2,1,0:T(8,128)(2,1)S(1)}, bf16[32,16,256]{2,1,0:T(8,128)(2,1)}, u32[]{:S(2)}) copy-start(bf16[32,16,256]{2,1,0:T(8,128)(2,1)} %param.21) | copy-start | bytes 786436
  391.2 77.6 %copy-start.1 = (bf16[512,2560]{1,0:T(8,128)(2,1)S(1)}, bf16[512,2560]{1,0:T(8,128)(2,1)}, u32[]{:S(2)}) copy-start(bf16[512,2560]{1,0:T(8,128)(2,1)} %param.25) | copy-start | bytes 7864324
  402.0 66.8 %copy-start.6 = (bf16[32,16,256]{2,1,0:T(8,128)(2,1)}, bf16[32,16,256]{2,1,0:T(8,128)(2,1)S(1)}, u32[]{:S(2)}) copy-start(bf16[32,16,256]{2,1,0:T(8,128)(2,1)S(1)} %scatter_fusion) | copy-start | bytes 786436
Sparse Core Ops, SparseCore 0:
  42.2 28.5 reduce-scatter.9
  74.6 86.6 all-gather.3
  303.2 83.7 reduce-scatter.11
  396.4 70.5 reduce-scatter.7
